TPU v7x, 32 devices: a whole 2x2x4 slice. The times are simulated.
32 devices in a mesh: dp: 4 (over z), span: 2 (over core), tensor: 4 (over y, x).
Axes of the slice: x: 2, y: 2, z: 4, core: 2. Of those that a mesh axis runs over, the one named last changes fastest.
Arguments:
- layer_input: bfloat16 [2, 16, 512, 768], P('span', 'dp', 'tensor'), may hold values from -6 to 6
- skip_tokens: bfloat16 [2, 16, 512, 768], P('span', 'dp', 'tensor'), may hold values from -6 to 6
- backbone_cotangent: bfloat16 [2, 16, 512, 768], P('span', 'dp', 'tensor'), may hold values from -6 to 6
- head_cotangent: bfloat16 [2, 16, 512, 768], P('span', 'dp', 'tensor'), may hold values from -6 to 6
- segment_lengths: int32 [2, 16, 4], P('span', 'dp'), may hold values from 1 to 174, 464 in all within a row
- pair_index: int32 [64], replicated, may hold values from 0 to 63, each once
- w_heads: bfloat16 [2, 3, 768, 768], P(None, None, None, 'tensor'), may hold values from -0.21875 to 0.21875
- heads_bias: bfloat16 [2, 2, 768], P(None, None, 'tensor'), may hold values from -1.75 to 1.75
- w_project: bfloat16 [2, 768, 768], P(None, 'tensor'), may hold values from -0.875 to 0.875
- project_bias: bfloat16 [2, 768], replicated, may hold values from -1.75 to 1.75
- norm_gain: bfloat16 [2, 2, 768], replicated, may hold values from 0.5 to 1.5
- norm_shift: bfloat16 [2, 2, 768], replicated, may hold values from -1.75 to 1.75
- w_expand: bfloat16 [2, 768, 3072], P(None, None, 'tensor'), may hold values from -0.21875 to 0.21875
- expand_bias: bfloat16 [2, 3072], P(None, 'tensor'), may hold values from -3 to 3
- w_shrink: bfloat16 [2, 3072, 768], P(None, 'tensor'), may hold values from -0.109375 to 0.109375
- shrink_bias: bfloat16 [2, 768], replicated, may hold values from -1.75 to 1.75
Outputs:
- backbone_out: bfloat16 [2, 16, 512, 768], P('span', 'dp', 'tensor')
- head_out: bfloat16 [2, 16, 512, 768], P('span', 'dp', 'tensor')
- span_loss: float32 [], replicated
- grad_input: bfloat16 [2, 16, 512, 768], P('span', 'dp', 'tensor')
- grad_skip: bfloat16 [2, 16, 512, 768], P('span', 'dp', 'tensor')
- grad_heads: float32 [2, 3, 768, 768], P(None, None, None, 'tensor')
- grad_heads_bias: float32 [2, 2, 768], P(None, None, 'tensor')
- grad_project: float32 [2, 768, 768], P(None, 'tensor')
- grad_project_bias: float32 [2, 768], replicated
- grad_gain: float32 [2, 2, 768], replicated
- grad_shift: float32 [2, 2, 768], replicated
- grad_expand: float32 [2, 768, 3072], P(None, None, 'tensor')
- grad_expand_bias: float32 [2, 3072], P(None, 'tensor')
- grad_shrink: float32 [2, 3072, 768], P(None, 'tensor')
- grad_shrink_bias: float32 [2, 768], replicated
Inputs may be any that keep to these rules, and one draw needn't show every extreme that they name: `segment_lengths`: each row holds 4 spans whose lengths add up to 464, the longest being 174; the rest of the row is padding. `pair_index`: each value occurs exactly once.
All inputs are finite; a program needn't handle non-finite values.
Results may differ from a plain program's by a relative error of at most 0.015.
The roundings to bfloat16 on the way count: a program that leaves them out, or rounds other values in their place, can miss the bound.
Values may be sent and summed in bfloat16 or wider, within the bound.
A program may use at most 192 MiB of HBM per device.

v0:
```python
import math
import jax
import jax.numpy as jnp
from jax import lax
from jax.sharding import PartitionSpec as P

HEAD_DIM = 64
EPSILON = 1e-12
LOSS_WEIGHT = 8.0
HIGHEST = lax.Precision.HIGHEST
MASKED = -1e30
BF = jnp.bfloat16
F32 = jnp.float32
BOTH = ("span", "tensor")


def mm(a, b, ca, cb):
    return lax.dot_general(a, b, (((ca,), (cb,)), ((), ())), preferred_element_type=F32)


def normal_parts(values):
    centred = values - jnp.mean(values, axis=-1, keepdims=True)
    spread = jnp.mean(centred * centred, axis=-1, keepdims=True)
    scale = lax.rsqrt(spread + EPSILON)
    return (centred * scale, scale)


def normal_back(upward, normed, scale, gain):
    weighted = upward * gain
    first = jnp.mean(weighted, axis=-1, keepdims=True)
    second = jnp.mean(weighted * normed, axis=-1, keepdims=True)
    return (weighted - first - normed * second) * scale


def split_heads(values):
    return values.reshape(values.shape[0], values.shape[1] // HEAD_DIM, HEAD_DIM)


def attend_forward(queries, keys, values, same):
    scores = (
        jnp.einsum(
            "qhd,khd->hqk", split_heads(queries), split_heads(keys), preferred_element_type=F32
        )
        * 0.125
    )
    scores = jnp.where(same[None], scores, MASKED)
    maximum = jnp.max(scores, axis=-1, keepdims=True)
    raised = jnp.exp(scores - maximum)
    total = jnp.sum(raised, axis=-1, keepdims=True)
    attention = (raised / total).astype(BF)
    mixture = jnp.einsum("hqk,khd->qhd", attention, split_heads(values), preferred_element_type=F32)
    return (mixture.reshape(queries.shape).astype(BF), maximum + jnp.log(total))


def attend_backward(queries, keys, values, same, upward, log_total):
    qh, kh, vh, uh = (split_heads(m) for m in (queries, keys, values, upward))
    scores = jnp.einsum("qhd,khd->hqk", qh, kh, preferred_element_type=F32) * 0.125
    scores = jnp.where(same[None], scores, MASKED)
    attention = jnp.exp(scores - log_total)
    grad_weights = jnp.einsum("qhd,khd->hqk", uh, vh, preferred_element_type=F32)
    inner = jnp.sum(attention * grad_weights, axis=-1, keepdims=True)
    grad_scores = (attention * (grad_weights - inner)).astype(BF)
    dq = jnp.einsum("hqk,khd->qhd", grad_scores, kh, preferred_element_type=F32) * 0.125
    dk = jnp.einsum("hqk,qhd->khd", grad_scores, qh, preferred_element_type=F32) * 0.125
    dv = jnp.einsum("hqk,qhd->khd", attention.astype(BF), uh, preferred_element_type=F32)
    return tuple((m.reshape(queries.shape).astype(BF) for m in (dq, dk, dv)))


def gelu_parts(hidden):
    phi = 0.5 * (1.0 + lax.erf(hidden * math.sqrt(0.5)))
    slope = phi + hidden * jnp.exp(-0.5 * hidden * hidden) * (1.0 / math.sqrt(2.0 * math.pi))
    return (hidden * phi, slope)


def layer_forward(x, same, attn_w, ffn_w, vec):
    wq, wk, wv, wp = attn_w
    we, ws = ffn_w
    xb = x.astype(BF)
    q = (mm(xb, wq, 1, 1) + vec["qb"]).astype(BF)
    k = mm(xb, wk, 1, 1).astype(BF)
    v = (mm(xb, wv, 1, 1) + vec["vb"]).astype(BF)
    o, lse = attend_forward(q, k, v, same)
    z1 = x + mm(o, wp, 1, 0) + vec["pb"]
    n1, r1 = normal_parts(z1)
    y = n1 * vec["g0"] + vec["s0"]
    yb = y.astype(BF)
    hid = jnp.einsum("qd,tdf->tqf", yb, we, preferred_element_type=F32) + vec["eb"][:, None, :]
    act, slope = gelu_parts(hid)
    act = act.astype(BF)
    z2 = y + jnp.einsum("tqf,tfd->qd", act, ws, preferred_element_type=F32) + vec["sb"]
    n2, r2 = normal_parts(z2)
    out = n2 * vec["g1"] + vec["s1"]
    return (out, (xb, q, k, v, o, lse, n1, r1, yb, act, slope.astype(BF), n2, r2))


def layer_backward(dout, same, attn_w, ffn_w, vec, kept):
    wq, wk, wv, wp = attn_w
    we, ws = ffn_w
    xb, q, k, v, o, lse, n1, r1, yb, act, slope, n2, r2 = kept
    dz2 = normal_back(dout, n2, r2, vec["g1"])
    dgain1 = jnp.sum(dout * n2, axis=0)
    dshift1 = jnp.sum(dout, axis=0)
    dsb = jnp.sum(dz2, axis=0)
    dzb = dz2.astype(BF)
    dws = jnp.einsum("tqf,qd->tfd", act, dzb, preferred_element_type=F32).astype(BF)
    dact = jnp.einsum("qd,tfd->tqf", dzb, ws, preferred_element_type=F32)
    dhid = dact * slope.astype(F32)
    deb = jnp.sum(dhid, axis=1)
    dhb = dhid.astype(BF)
    dwe = jnp.einsum("qd,tqf->tdf", yb, dhb, preferred_element_type=F32).astype(BF)
    dy = dz2 + jnp.einsum("tqf,tdf->qd", dhb, we, preferred_element_type=F32)
    dz1 = normal_back(dy, n1, r1, vec["g0"])
    dgain0 = jnp.sum(dy * n1, axis=0)
    dshift0 = jnp.sum(dy, axis=0)
    dpb = jnp.sum(dz1, axis=0)
    da = dz1.astype(BF)
    dwp = mm(o, da, 0, 0).astype(BF)
    do = mm(da, wp, 1, 1).astype(BF)
    dq, dk, dv = attend_backward(q, k, v, same, do, lse)
    dwq = mm(dq, xb, 0, 0).astype(BF)
    dwk = mm(dk, xb, 0, 0).astype(BF)
    dwv = mm(dv, xb, 0, 0).astype(BF)
    dqb = jnp.sum(dq.astype(F32), axis=0)
    dvb = jnp.sum(dv.astype(F32), axis=0)
    dx = dz1 + mm(dq, wq, 1, 0) + mm(dk, wk, 1, 0) + mm(dv, wv, 1, 0)
    small = {
        "qb": dqb,
        "vb": dvb,
        "pb": dpb,
        "g0": dgain0,
        "g1": dgain1,
        "s0": dshift0,
        "s1": dshift1,
        "sb": dsb,
        "eb": deb.reshape(-1),
    }
    return (dx, (dwq, dwk, dwv, dwp), (dwe, dws), small)


SMALL = ("qb", "vb", "pb", "g0", "g1", "s0", "s1", "sb", "eb")


def to_rows(values):
    return lax.all_to_all(values, "tensor", split_axis=0, concat_axis=1, tiled=True)[0]


def to_places(values):
    return lax.all_to_all(values[None], "tensor", split_axis=1, concat_axis=0, tiled=True)


def shards(
    layer_input,
    skip_tokens,
    backbone_cotangent,
    head_cotangent,
    segment_lengths,
    pair_index,
    w_heads,
    heads_bias,
    w_project,
    project_bias,
    norm_gain,
    norm_shift,
    w_expand,
    expand_bias,
    w_shrink,
    shrink_bias,
):
    side = lax.axis_index("span")
    mine = lax.axis_index("tensor")
    tensor_count = lax.axis_size("tensor")
    width = layer_input.shape[-1]
    head_cols = w_heads.shape[-1]
    ff_cols = w_expand.shape[-1]

    def gather_attn(l):
        heads = jnp.swapaxes(w_heads[l], 1, 2)
        zero = jnp.stack([heads[0], heads[1]])
        one = jnp.stack([heads[2], w_project[l]])
        got = lax.all_gather(jnp.where(side == 0, zero, one), BOTH, axis=0, tiled=False)
        got = got.reshape(2, tensor_count, 2, head_cols, width)
        return tuple(
            (
                got[i, :, j].reshape(tensor_count * head_cols, width)
                for i in range(2)
                for j in range(2)
            )
        )

    def gather_ffn(l):
        got = lax.all_gather(
            jnp.where(side == 0, w_expand[l], w_shrink[l]), BOTH, axis=0, tiled=False
        )
        got = got.reshape(2, tensor_count, width, ff_cols)
        return (got[0], got[1])

    small_in = jnp.concatenate([heads_bias.reshape(-1), expand_bias.reshape(-1)])
    small_got = lax.all_gather(small_in, "tensor", axis=0, tiled=False).astype(F32)
    hb_all = jnp.transpose(
        small_got[:, : 4 * head_cols].reshape(tensor_count, 2, 2, head_cols), (1, 2, 0, 3)
    )
    hb_all = hb_all.reshape(2, 2, tensor_count * head_cols)
    eb_all = jnp.transpose(
        small_got[:, 4 * head_cols :].reshape(tensor_count, 2, ff_cols), (1, 0, 2)
    )

    def vectors(l):
        return {
            "qb": hb_all[l, 0],
            "vb": hb_all[l, 1],
            "pb": project_bias[l].astype(F32),
            "g0": norm_gain[l, 0].astype(F32),
            "g1": norm_gain[l, 1].astype(F32),
            "s0": norm_shift[l, 0].astype(F32),
            "s1": norm_shift[l, 1].astype(F32),
            "sb": shrink_bias[l].astype(F32),
            "eb": eb_all[l],
        }

    attn_w0 = gather_attn(0)
    ffn_w0 = gather_ffn(0)
    attn_w1 = gather_attn(1)
    ffn_w1 = gather_ffn(1)
    x = to_rows(layer_input[0])
    skip = to_rows(skip_tokens[0])
    backbone_cot = to_rows(backbone_cotangent[0])
    head_cot = to_rows(head_cotangent[0])
    tokens = x.shape[0]
    lengths = lax.dynamic_index_in_dim(segment_lengths[0], mine, 0, keepdims=False)
    span_count = lengths.shape[0]
    starts = jnp.cumsum(lengths) - lengths
    row_length = jnp.sum(lengths)
    places = jnp.arange(tokens, dtype=jnp.int32)
    counted = jnp.sum((places[:, None] >= starts[None, :]).astype(jnp.int32), axis=-1) - 1
    segment = jnp.where(places < row_length, counted, span_count)
    same = segment[:, None] == segment[None, :]
    valid = (places < row_length).astype(F32)[:, None]
    picker = (starts[:, None] == places[None, :]).astype(F32)
    first = jnp.sum(picker, axis=0)[:, None] > 0
    vec0, vec1 = (vectors(0), vectors(1))
    backbone, kept0 = layer_forward(x.astype(F32), same, attn_w0, ffn_w0, vec0)
    cls = mm(picker.astype(BF), backbone.astype(BF), 1, 0).astype(BF)
    anchors = lax.all_gather(cls, ("dp", "span", "tensor"), axis=0, tiled=False)
    dp_count = lax.axis_size("dp")
    pair_count = lax.axis_size("span")
    anchors = anchors.reshape(dp_count, pair_count, tensor_count * span_count, width)
    anchors = jnp.swapaxes(anchors, 0, 1).reshape(
        pair_count, dp_count * tensor_count * span_count, width
    )
    head_in = jnp.where(first, backbone, skip.astype(F32))
    head, kept1 = layer_forward(head_in, same, attn_w1, ffn_w1, vec1)
    vector_count = anchors.shape[1]
    root = math.sqrt(width)
    logits = mm(anchors[0], anchors[1], 1, 1) / root
    columns = jnp.arange(vector_count, dtype=jnp.int32)
    target = (pair_index[:, None] == columns[None, :]).astype(F32)
    lse_rows = jax.nn.logsumexp(logits, axis=1)
    lse_cols = jax.nn.logsumexp(logits, axis=0)
    dlogits = LOSS_WEIGHT * (
        jnp.exp(logits - lse_rows[:, None]) + jnp.exp(logits - lse_cols[None, :]) - 2.0 * target
    )
    span_loss = (jnp.sum(lse_rows) + jnp.sum(lse_cols) - 2.0 * jnp.sum(target * logits)) / (
        2 * vector_count
    )
    own = (lax.axis_index("dp") * tensor_count + mine) * span_count
    wanted = jnp.where(side == 0, dlogits, dlogits.T)
    wanted = lax.dynamic_slice(wanted, (own, 0), (span_count, vector_count))
    other = lax.dynamic_index_in_dim(anchors, 1 - side, 0, keepdims=False).astype(F32)
    dcls = jnp.dot(wanted, other, precision=HIGHEST) / root
    du, dattn1, dffn1, small1 = layer_backward(
        head_cot.astype(F32) * valid, same, attn_w1, ffn_w1, vec1, kept1
    )
    grad_skip = jnp.where(first, 0.0, du).astype(BF)
    seed = backbone_cot.astype(F32) * valid + jnp.where(first, du, 0.0)
    seed = seed + jnp.dot(picker.T, dcls, precision=HIGHEST)
    dx, dattn0, dffn0, small0 = layer_backward(seed, same, attn_w0, ffn_w0, vec0, kept0)

    def reduce_attn(grads):
        packed = jnp.stack([g.reshape(tensor_count, head_cols, width) for g in grads])
        packed = packed.reshape(2, 2, tensor_count, head_cols, width)
        packed = jnp.swapaxes(packed, 1, 2).reshape(2 * tensor_count, 2, head_cols, width)
        part = lax.psum_scatter(packed, BOTH, scatter_dimension=0, tiled=False)
        part = lax.psum(part, "dp")
        got = lax.all_gather(part, "span", axis=0, tiled=False).astype(F32)
        heads = jnp.stack([got[0, 0], got[0, 1], got[1, 0]])
        return (jnp.swapaxes(heads, 1, 2), got[1, 1])

    def reduce_ffn(grads):
        packed = jnp.stack(grads).reshape(2 * tensor_count, width, ff_cols)
        part = lax.psum_scatter(packed, BOTH, scatter_dimension=0, tiled=False)
        part = lax.psum(part, "dp")
        got = lax.all_gather(part, "span", axis=0, tiled=False).astype(F32)
        return (got[0], got[1])

    ge1, gs1 = reduce_ffn(dffn1)
    gh1, gp1 = reduce_attn(dattn1)
    ge0, gs0 = reduce_ffn(dffn0)
    gh0, gp0 = reduce_attn(dattn0)
    flat = jnp.concatenate([small[k] for small in (small0, small1) for k in SMALL])
    flat = lax.psum(flat, ("dp", "span", "tensor"))
    sizes = [small0[k].shape[0] for k in SMALL] * 2
    cuts = []
    at = 0
    for size in sizes:
        cuts.append(flat[at : at + size])
        at += size
    s0 = dict(zip(SMALL, cuts[: len(SMALL)]))
    s1 = dict(zip(SMALL, cuts[len(SMALL) :]))

    def local(values, size):
        return lax.dynamic_slice(values, (mine * size,), (size,))

    hb = jnp.stack(
        [jnp.stack([local(s["qb"], head_cols), local(s["vb"], head_cols)]) for s in (s0, s1)]
    )
    eb = jnp.stack([local(s["eb"], ff_cols) for s in (s0, s1)])
    return (
        to_places((backbone * valid).astype(BF))[None],
        to_places((head * valid).astype(BF))[None],
        span_loss,
        to_places(dx.astype(BF))[None],
        to_places(grad_skip)[None],
        jnp.stack([gh0, gh1]),
        hb,
        jnp.stack([gp0, gp1]),
        jnp.stack([s0["pb"], s1["pb"]]),
        jnp.stack([jnp.stack([s["g0"], s["g1"]]) for s in (s0, s1)]),
        jnp.stack([jnp.stack([s["s0"], s["s1"]]) for s in (s0, s1)]),
        jnp.stack([ge0, ge1]),
        eb,
        jnp.stack([gs0, gs1]),
        jnp.stack([s0["sb"], s1["sb"]]),
    )


def solution(mesh):
    rows = P("span", "dp", "tensor", None)
    in_specs = (
        rows,
        rows,
        rows,
        rows,
        P("span", "dp", None),
        P(),
        P(None, None, None, "tensor"),
        P(None, None, "tensor"),
        P(None, "tensor", None),
        P(),
        P(),
        P(),
        P(None, None, "tensor"),
        P(None, "tensor"),
        P(None, "tensor", None),
        P(),
    )
    out_specs = (
        rows,
        rows,
        P(),
        rows,
        rows,
        P(None, None, None, "tensor"),
        P(None, None, "tensor"),
        P(None, "tensor", None),
        P(),
        P(),
        P(),
        P(None, None, "tensor"),
        P(None, "tensor"),
        P(None, "tensor", None),
        P(),
    )
    return jax.shard_map(shards, mesh=mesh, in_specs=in_specs, out_specs=out_specs, check_vma=False)
```

profile of v0, /device:TPU:0, one launch (start us, length us, event | category | flops | bytes accessed | tf_op | source)
XLA Modules:
  0.0 985.8 jit_solution(689958023518793474)
XLA Ops:
  12.7 3.3 slice_select_fusion
  16.1 5.3 all-to-all-start.5
  25.8 16.1 %all-gather.4 = bf16[4,1,2304]{2,1,0:T(2,128)(2,1)S(1)} all-gather(bf16[1,1,2304]{2,1,0:T(2,128)(2,1)S(1)} %reshape.546), channel_id=3, replica_groups=mesh['dp'=4,'span'=2,'tensor'=4] {'tensor'}, dimensions={0}, use_global_device_ids=true | all-gather | bytes 23040 | tf_op jit(solution)/shard_map/all_gather | solution.py:198
  44.3 3.5 all-to-all-start
  49.3 20.0 %all-gather.27.cloned.1.call-done = bf16[16,192,768]{2,1,0:T(8,128)(2,1)} async-done(((bf16[2,192,768]{2,1,0:T(8,128)(2,1)}), bf16[16,192,768]{2,1,0:T(8,128)(2,1)}) %all-gather.27.cloned.1.call-update) | async-done | bytes 4718608 | tf_op jit(solution)/shard_map/all_gather | solution.py:180
  69.3 4.2 fusion.150
  73.5 4.4 all-to-all-start.2
  86.4 2.6 fusion
  90.9 3.6 fusion.69
  96.6 21.1 %all-gather.29.cloned.1.call-done = bf16[16,192,768]{2,1,0:T(8,128)(2,1)} async-done(((bf16[2,192,768]{2,1,0:T(8,128)(2,1)}), bf16[16,192,768]{2,1,0:T(8,128)(2,1)}) %all-gather.29.cloned.1.call-update) | async-done | bytes 4718608 | tf_op jit(solution)/shard_map/all_gather | solution.py:180
  117.7 4.6 fusion.149
  122.4 56.6 %all-gather.15.cloned.1.call-done = bf16[8,768,768]{2,1,0:T(8,128)(2,1)} async-done(((bf16[1,768,768]{2,1,0:T(8,128)(2,1)}), bf16[8,768,768]{2,1,0:T(8,128)(2,1)}) %all-gather.15.cloned.1.call-update) | async-done | bytes 9437200 | tf_op jit(solution)/shard_map/all_gather | solution.py:191
  178.9 7.4 fusion.25
  186.4 2.8 fusion.158
  189.9 69.3 %all-gather.5 = bf16[32,4,768]{2,1,0:T(4,128)(2,1)S(1)} all-gather(bf16[1,4,768]{2,1,0:T(4,128)(2,1)S(1)} %fusion.74), channel_id=5, replica_groups=mesh['dp'=4,'span'=2,'tensor'=4] {'dp','span','tensor'}, dimensions={0}, use_global_device_ids=true | all-gather | bytes 202752 | tf_op jit(solution)/shard_map/all_gather | solution.py:243
  260.0 4.2 all-to-all-start.4
  264.3 2.6 fusion.75
  270.9 2.6 add_convert_fusion.2
  274.7 3.2 convolution_convert_fusion.10
  283.1 2.6 fusion.1
  287.6 3.8 fusion.68
  291.4 2.5 fusion.159
  295.3 5.5 fusion.21
  300.8 2.8 fusion.160
  308.3 4.9 fusion.36
  313.2 9.8 multiply_reduce_fusion.3
  323.0 2.6 fusion.143
  331.5 9.6 convert_reduce_fusion
  341.1 9.7 multiply_reduce_fusion.1
  350.7 7.1 multiply_convert_fusion.1
  372.9 2.6 copy.201
  377.4 4.7 add_add_fusion
  382.1 4.0 multiply_reduce_fusion.4
  386.9 8.0 fusion.38
  394.9 3.1 multiply_reduce_fusion.5
  404.0 8.3 convert_reduce_fusion.2
  414.0 11.2 %multiply_reduce_fusion = (f32[12,512]{1,0:T(8,128)S(1)}, f32[12,512,512]{1,2,0:T(8,128)}) fusion(f32[12,512]{1,0:T(8,128)S(1)} %copy-done.66, f32[12,512,512]{1,2,0:T(8,128)} %copy-done, pred[512,512]{0,1:T(8,128)(4,1)S(1)} %broadcast_compare_fusion, bf16[512,12,64]{0,2,1:T(8,128)(2,1)S(1)} %bitcast.409, bf16[512,12,64]{0,2,1:T(8,128)(2,1)S(1)} %bitcast.439), kind=kOutput, calls=%fused_computation.1 | convolution fusion | flops 418375680 | bytes 27049984 | tf_op jit(solution)/shard_map/qhd,khd->hqk/dot_general | solution.py:60
  425.5 7.1 multiply_convert_fusion
  440.1 2.6 copy.200
  443.1 7.4 convert_bitcast_fusion
  450.5 8.4 convert_bitcast_fusion.1
  458.9 8.4 pad_maximum_fusion.1
  467.3 12.7 %copy.209 = bf16[8,768,768]{2,1,0:T(8,128)(2,1)} copy(bf16[8,768,768]{1,2,0:T(8,128)(2,1)} %bitcast.378) | data formatting | bytes 18874368 | tf_op jit(solution)/shard_map/reshape | solution.py:289
  480.5 7.3 convert_bitcast_fusion.2
  487.9 7.7 convert_bitcast_fusion.3
  495.6 8.3 pad_maximum_fusion
  503.9 13.5 %copy.205 = bf16[8,768,768]{2,1,0:T(8,128)(2,1)} copy(bf16[8,768,768]{1,2,0:T(8,128)(2,1)} %bitcast.379) | data formatting | bytes 18874368 | tf_op jit(solution)/shard_map/reshape | solution.py:289
  517.5 58.3 %reduce-scatter.11.cloned.1.call-done = bf16[1,768,768]{2,1,0:T(8,128)(2,1)} async-done(((bf16[8,768,768]{2,1,0:T(8,128)(2,1)}), bf16[1,768,768]{2,1,0:T(8,128)(2,1)}) %reduce-scatter.11.cloned.1.call-update) | async-done | bytes 1179664 | tf_op jit(solution)/shard_map/reduce_scatter | solution.py:290
  575.7 80.3 %reduce-scatter.9.cloned.1.call-done = bf16[1,768,768]{2,1,0:T(8,128)(2,1)} async-done(((bf16[8,768,768]{2,1,0:T(8,128)(2,1)}), bf16[1,768,768]{2,1,0:T(8,128)(2,1)}) %reduce-scatter.9.cloned.1.call-update) | async-done | bytes 1179664 | tf_op jit(solution)/shard_map/reduce_scatter | solution.py:290
  658.1 134.5 %all-reduce.6.cloned.1.call-done = (bf16[1,2,192,768]{3,2,1,0:T(8,128)(2,1)}, bf16[1,2,192,768]{3,2,1,0:T(8,128)(2,1)}, bf16[1,768,768]{2,1,0:T(8,128)(2,1)}, bf16[1,768,768]{2,1,0:T(8,128)(2,1)}) async-done(((bf16[1,2,192,768]{3,2,1,0:T(8,128)(2,1)}, bf16[1,2,192,768]{3,2,1,0:T(8,128)(2,1)}, bf16[1,768,768]{2,1,0:T(8,128)(2,1)}, bf16[1,768,768]{2,1,0:T(8,128)(2,1)}), (bf16[1,2,192,768]{3,2,1,0:T(8,128)(2,1)}, ...) | async-done | bytes 3538960 | tf_op jit(solution)/shard_map/psum | solution.py:283
  796.1 6.3 reduce.44
  804.3 4.2 all-to-all-start.1
  811.1 6.3 reduce.45
  823.6 4.6 all-to-all-start.3
  830.3 5.4 reduce.47
  838.2 5.4 reduce.46
  847.2 71.1 %all-reduce.4.cloned.1.call-done = f32[18432]{0:T(1024)} async-done(((f32[18432]{0:T(1024)}), f32[18432]{0:T(1024)}) %all-reduce.4.cloned.1.call-update) | async-done | bytes 73744 | tf_op jit(solution)/shard_map/psum | solution.py:300
  920.0 3.5 all-to-all-start.7
  925.2 10.3 %all-to-all-done.7 = bf16[4,2,49152]{2,1,0:T(2,128)(2,1)S(1)} async-done(((bf16[4,2,49152]{2,1,0:T(2,128)(2,1)}), bf16[4,2,49152]{2,1,0:T(2,128)(2,1)S(1)}, u32[]{:S(2)}, u32[]{:S(2)}) %all-to-all-start.7) | async-done | bytes 786464 | tf_op jit(solution)/shard_map/all_to_all | solution.py:148
  935.5 3.5 all-to-all-start.6
  958.9 3.4 fusion.151
  962.3 8.0 all-gather.25.cloned.1.call-done
  972.7 2.5 pad_maximum_fusion.5
  975.2 2.5 pad_maximum_fusion.4
  (470 shorter events, 132.9 us)
Async XLA Ops:
  7.2 62.2 %all-gather.27.cloned.1.call-start = ((), (), s32[]{:S(2)}) async-start(), calls=%async_computation.23 | async-start | bytes 5308416 | tf_op jit(solution)/shard_map/all_gather | solution.py:180
  10.8 106.9 %all-gather.29.cloned.1.call-start = ((), (), s32[]{:S(2)}) async-start(), calls=%async_computation.24 | async-start | bytes 5308416 | tf_op jit(solution)/shard_map/all_gather | solution.py:180
  11.8 167.1 %all-gather.15.cloned.1.call-start = ((), (), s32[]{:S(2)}) async-start(), calls=%async_computation.12 | async-start | bytes 10616832 | tf_op jit(solution)/shard_map/all_gather | solution.py:191
  16.0 8.3 copy-start.101
  16.0 8.4 copy-start.100
  16.0 8.5 copy-start.91
  16.0 9.0 copy-start.81
  16.1 9.1 copy-start.82
  16.1 9.7 copy-start.69
  16.1 26.7 %copy-start.70 = (bf16[2,2,768]{2,1,0:T(2,128)(2,1)S(1)}, bf16[2,2,768]{2,1,0:T(2,128)(2,1)}, u32[]{:S(2)}) copy-start(bf16[2,2,768]{2,1,0:T(2,128)(2,1)} %param.27) | copy-start | bytes 18436
  16.1 28.2 %all-to-all-start.5 = ((bf16[4,128,768]{2,1,0:T(8,128)(2,1)}), bf16[4,128,768]{2,1,0:T(8,128)(2,1)S(1)}, u32[]{:S(2)}, u32[]{:S(2)}) async-start(bf16[4,128,768]{2,1,0:T(8,128)(2,1)} %bitcast.446), calls=%async_computation.5 | async-start | bytes 1572864 | tf_op jit(solution)/shard_map/all_to_all | solution.py:144
  21.4 273.8 %all-gather.17.cloned.1.call-start = ((), (), s32[]{:S(2)}) async-start(), calls=%async_computation.13 | async-start | bytes 10616832 | tf_op jit(solution)/shard_map/all_gather | solution.py:191
  22.8 166.7 %copy-start.88 = (s32[4]{0:T(128)}, s32[4]{0:T(128)S(1)}, u32[]{:S(2)}) copy-start(s32[4]{0:T(128)S(1)} %bitcast_subtract_fusion) | copy-start | bytes 52
  23.7 267.7 %copy-start.94 = (pred[512]{0:T(512)(128)(4,1)}, pred[512]{0:T(512)(128)(4,1)S(1)}, u32[]{:S(2)}) copy-start(pred[512]{0:T(512)(128)(4,1)S(1)} %broadcast_compare_fusion.1) | copy-start | bytes 1540
  43.4 142.9 %copy-start.77 = (f32[768]{0:T(1024)}, f32[768]{0:T(1024)S(1)}, u32[]{:S(2)}) copy-start(f32[768]{0:T(1024)S(1)} %get-tuple-element.45) | copy-start | bytes 9220
  44.0 134.9 %copy-start.84 = (f32[4,768]{1,0:T(4,128)}, f32[4,768]{1,0:T(4,128)S(1)}, u32[]{:S(2)}) copy-start(f32[4,768]{1,0:T(4,128)S(1)} %get-tuple-element.121) | copy-start | bytes 36868
  44.3 29.3 %copy-start.6 = (bf16[4,128,768]{2,1,0:T(8,128)(2,1)}, bf16[4,128,768]{2,1,0:T(8,128)(2,1)S(1)}, u32[]{:S(2)}) copy-start(bf16[4,128,768]{2,1,0:T(8,128)(2,1)S(1)} %all-to-all-done.5) | copy-start | bytes 2359300
  44.3 29.3 %all-to-all-start = ((bf16[4,128,768]{2,1,0:T(8,128)(2,1)}), bf16[4,128,768]{2,1,0:T(8,128)(2,1)S(1)}, u32[]{:S(2)}, u32[]{:S(2)}) async-start(bf16[4,128,768]{2,1,0:T(8,128)(2,1)} %bitcast), calls=%async_computation | async-start | bytes 1572864 | tf_op jit(solution)/shard_map/all_to_all | solution.py:144
  73.5 9.0 copy-start.18
  73.5 186.5 %all-to-all-start.2 = ((bf16[4,128,768]{2,1,0:T(8,128)(2,1)}), bf16[4,128,768]{2,1,0:T(8,128)(2,1)}, u32[]{:S(2)}, u32[]{:S(2)}) async-start(bf16[4,128,768]{2,1,0:T(8,128)(2,1)} %bitcast.29), calls=%async_computation.2 | async-start | bytes 1572864 | tf_op jit(solution)/shard_map/all_to_all | solution.py:144
  95.5 90.8 %copy-start.2 = (f32[512,768]{1,0:T(8,128)}, f32[512,768]{1,0:T(8,128)S(1)}, u32[]{:S(2)}) copy-start(f32[512,768]{1,0:T(8,128)S(1)} %get-tuple-element.127) | copy-start | bytes 4718596
  178.9 7.4 copy-start.103
  259.3 7.6 copy-start.34
  260.0 122.0 %all-to-all-start.4 = ((bf16[4,128,768]{2,1,0:T(8,128)(2,1)}), bf16[4,128,768]{2,1,0:T(8,128)(2,1)}, u32[]{:S(2)}, u32[]{:S(2)}) async-start(bf16[4,128,768]{2,1,0:T(8,128)(2,1)} %bitcast.54), calls=%async_computation.4 | async-start | bytes 1572864 | tf_op jit(solution)/shard_map/all_to_all | solution.py:144
  264.3 253.2 %reduce-scatter.7.cloned.1.call-start = ((), (), s32[]{:S(2)}) async-start(), calls=%async_computation.16 | async-start | bytes 5308416 | tf_op jit(solution)/shard_map/reduce_scatter | solution.py:282
  270.9 10.1 %copy-start.11 = (bf16[512,768]{0,1:T(8,128)(2,1)}, bf16[512,768]{0,1:T(8,128)(2,1)S(1)}, u32[]{:S(2)}) copy-start(bf16[512,768]{0,1:T(8,128)(2,1)S(1)} %copy.183) | copy-start | bytes 2359300
  280.8 14.3 %copy-start.48 = (f32[64,64]{1,0:T(8,128)}, f32[64,64]{1,0:T(8,128)S(1)}, u32[]{:S(2)}) copy-start(f32[64,64]{1,0:T(8,128)S(1)} %get-tuple-element.140) | copy-start | bytes 49156
  293.9 19.3 %copy-start.4 = (f32[512,768]{1,0:T(8,128)}, f32[512,768]{1,0:T(8,128)S(1)}, u32[]{:S(2)}) copy-start(f32[512,768]{1,0:T(8,128)S(1)} %get-tuple-element.135) | copy-start | bytes 4718596
  295.0 28.0 %copy-start.71 = (f32[512]{0:T(512)}, f32[512]{0:T(512)S(1)}, u32[]{:S(2)}) copy-start(f32[512]{0:T(512)S(1)} %add_rsqrt_fusion.1) | copy-start | bytes 6148
  313.2 9.8 copy-start.15
  313.2 9.8 copy-start.27
  331.5 9.6 copy-start.22
  331.5 9.6 copy-start.24
  331.5 19.2 %slice-start.3 = ((s8[12582912]{0:T(1024)(128)(4,1)}), s8[4194304]{0:T(1024)(128)(4,1)S(1)}, s32[]{:S(2)}) async-start(s8[12582912]{0:T(1024)(128)(4,1)} %bitcast.376), calls=%async_computation.29 | async-start | bytes 8388608
  331.5 19.2 %slice-start.4 = ((s8[12582912]{0:T(1024)(128)(4,1)}), s8[4194304]{0:T(1024)(128)(4,1)S(1)}, s32[]{:S(2)}) async-start(s8[12582912]{0:T(1024)(128)(4,1)} %bitcast.376), calls=%async_computation.30 | async-start | bytes 8388608
  341.1 9.7 slice-start.5
  375.5 142.0 %reduce-scatter.5.cloned.1.call-start = ((), (), s32[]{:S(2)}) async-start(), calls=%async_computation.14 | async-start | bytes 5308416 | tf_op jit(solution)/shard_map/reduce_scatter | solution.py:282
  382.1 12.8 %slice-start.6 = ((s8[9437184]{0:T(1024)(128)(4,1)}), s8[4194304]{0:T(1024)(128)(4,1)S(1)}, s32[]{:S(2)}) async-start(s8[9437184]{0:T(1024)(128)(4,1)} %bitcast.475), calls=%async_computation.32 | async-start | bytes 8388608
  386.7 8.2 copy-start.36
  386.9 8.0 copy-start.3
  386.9 8.1 slice-start.7
  386.9 8.1 slice-start.8
  404.0 9.2 copy-start.61
  404.0 10.0 %copy-start.23 = (bf16[512,768]{0,1:T(8,128)(2,1)S(1)}, bf16[512,768]{0,1:T(8,128)(2,1)}, u32[]{:S(2)}) copy-start(bf16[512,768]{0,1:T(8,128)(2,1)} %copy.194) | copy-start | bytes 2359300
  404.0 10.0 %copy-start.51 = (bf16[768,512]{1,0:T(8,128)(2,1)S(1)}, bf16[768,512]{1,0:T(8,128)(2,1)}, u32[]{:S(2)}) copy-start(bf16[768,512]{1,0:T(8,128)(2,1)} %add_convert_fusion.4) | copy-start | bytes 2359300
  413.2 12.0 %slice-start = ((s8[12582912]{0:T(1024)(128)(4,1)}), s8[4194304]{0:T(1024)(128)(4,1)S(1)}, s32[]{:S(2)}) async-start(s8[12582912]{0:T(1024)(128)(4,1)} %bitcast.374), calls=%async_computation.26 | async-start | bytes 8388608
  414.0 11.2 %slice-start.1 = ((s8[12582912]{0:T(1024)(128)(4,1)}), s8[4194304]{0:T(1024)(128)(4,1)S(1)}, s32[]{:S(2)}) async-start(s8[12582912]{0:T(1024)(128)(4,1)} %bitcast.374), calls=%async_computation.27 | async-start | bytes 8388608
  414.0 11.5 %slice-start.2 = ((s8[12582912]{0:T(1024)(128)(4,1)}), s8[4194304]{0:T(1024)(128)(4,1)S(1)}, s32[]{:S(2)}) async-start(s8[12582912]{0:T(1024)(128)(4,1)} %bitcast.374), calls=%async_computation.28 | async-start | bytes 8388608
  442.7 7.7 copy-start.72
  442.7 7.7 copy-start.80
  442.7 133.0 %reduce-scatter.11.cloned.1.call-start = ((), (), s32[]{:S(2)}) async-start(), calls=%async_computation.21 | async-start | bytes 10616832 | tf_op jit(solution)/shard_map/reduce_scatter | solution.py:290
  480.0 7.9 copy-start.78
  480.0 176.1 %reduce-scatter.9.cloned.1.call-start = ((), (), s32[]{:S(2)}) async-start(), calls=%async_computation.19 | async-start | bytes 10616832 | tf_op jit(solution)/shard_map/reduce_scatter | solution.py:290
  517.4 275.2 %all-reduce.6.cloned.1.call-start = ((), (), s32[]{:S(2)}) async-start(), calls=%async_computation.25 | async-start | bytes 7077888 | tf_op jit(solution)/shard_map/psum | solution.py:283
  656.2 262.2 %all-reduce.4.cloned.1.call-start = ((), (), s32[]{:S(2)}) async-start(), calls=%async_computation.18 | async-start | bytes 147456 | tf_op jit(solution)/shard_map/psum | solution.py:300
  658.0 294.1 %all-gather.19.cloned.1.call-start = ((), (), s32[]{:S(2)}) async-start(), calls=%async_computation.15 | async-start | bytes 1769472 | tf_op jit(solution)/shard_map/all_gather | solution.py:284
  792.6 161.1 %all-gather.21.cloned.1.call-start = ((), (), s32[]{:S(2)}) async-start(), calls=%async_computation.17 | async-start | bytes 1769472 | tf_op jit(solution)/shard_map/all_gather | solution.py:284
  804.3 19.2 %all-to-all-start.1 = ((bf16[4,2,49152]{2,1,0:T(2,128)(2,1)}), bf16[4,2,49152]{2,1,0:T(2,128)(2,1)}, u32[]{:S(2)}, u32[]{:S(2)}) async-start(bf16[4,2,49152]{2,1,0:T(2,128)(2,1)} %reshape.577), calls=%async_computation.1 | async-start | bytes 1572864 | tf_op jit(solution)/shard_map/all_to_all | solution.py:148
  808.5 150.4 %all-gather.23.cloned.1.call-start = ((), (), s32[]{:S(2)}) async-start(), calls=%async_computation.20 | async-start | bytes 3538944 | tf_op jit(solution)/shard_map/all_gather | solution.py:292
  823.6 96.4 %all-to-all-start.3 = ((bf16[4,2,49152]{2,1,0:T(2,128)(2,1)}), bf16[4,2,49152]{2,1,0:T(2,128)(2,1)}, u32[]{:S(2)}, u32[]{:S(2)}) async-start(bf16[4,2,49152]{2,1,0:T(2,128)(2,1)} %reshape.579), calls=%async_computation.3 | async-start | bytes 1572864 | tf_op jit(solution)/shard_map/all_to_all | solution.py:148
  838.2 7.7 copy-start.93
  920.0 15.5 %all-to-all-start.7 = ((bf16[4,2,49152]{2,1,0:T(2,128)(2,1)}), bf16[4,2,49152]{2,1,0:T(2,128)(2,1)S(1)}, u32[]{:S(2)}, u32[]{:S(2)}) async-start(bf16[4,2,49152]{2,1,0:T(2,128)(2,1)} %reshape.583), calls=%async_computation.7 | async-start | bytes 1572864 | tf_op jit(solution)/shard_map/all_to_all | solution.py:148
  923.5 46.8 %all-gather.25.cloned.1.call-start = ((), (), s32[]{:S(2)}) async-start(), calls=%async_computation.22 | async-start | bytes 3538944 | tf_op jit(solution)/shard_map/all_gather | solution.py:292
  935.5 14.9 %all-to-all-start.6 = ((bf16[4,2,49152]{2,1,0:T(2,128)(2,1)}), bf16[4,2,49152]{2,1,0:T(2,128)(2,1)S(1)}, u32[]{:S(2)}, u32[]{:S(2)}) async-start(bf16[4,2,49152]{2,1,0:T(2,128)(2,1)} %reshape.581), calls=%async_computation.6 | async-start | bytes 1572864 | tf_op jit(solution)/shard_map/all_to_all | solution.py:148
  (74 other events, 210.7 us)
Sparse Core Ops, SparseCore 0:
  11.0 58.3 all-gather.26
  71.8 45.9 all-gather.28
  120.2 58.6 all-gather.14
  181.2 60.4 all-gather.16
  375.6 52.3 reduce-scatter.6
  442.8 52.5 reduce-scatter.4
  498.9 76.8 reduce-scatter.10
  579.2 76.8 reduce-scatter.8
  658.7 133.8 all-reduce.5
  798.6 119.6 all-reduce.3
  919.9 11.2 all-gather.18
  932.6 10.3 all-gather.20
  944.6 12.1 all-gather.22
  958.1 12.1 all-gather.24
where the time goes:
time: 992 us; the launch traced here: 986 us
  waiting for transfers between devices  462 us (47%)
  matrix products  180 us (18%)
  local copies, waits for them, and re-layouts  102 us (10%)
  other arithmetic  102 us (10%)
  blocking collectives  85.4 us (9%)
  starting transfers between devices  34.9 us (4%)
  between operations  19.5 us (2%)
    reduce_scatter x2, waiting for transfers between devices, reduce_ffn(): part = lax.psum_scatter(packed, BOTH, scatter_dimension=0, tiled=False)  139 us
    psum x1, waiting for transfers between devices, reduce_attn(): part = lax.psum(part, 'dp')  135 us
    psum x1, waiting for transfers between devices, shards(): flat = lax.psum(flat, ('dp', 'span', 'tensor'))  71.1 us
    all_gather x1, blocking collectives, shards(): anchors = lax.all_gather(cls, ('dp', 'span', 'tensor'), axis=0, tiled=False)  69.3 us
    all_gather x2, waiting for transfers between devices, gather_ffn(): lax.all_gather(jnp.where(side == 0, w_expand[l], w_shrink[l]), BOTH, axis...  56.6 us
    dot_general x26, matrix products, mm(): lax.dot_general(a, b, (((ca,), (cb,)), ((), ())), preferred_element_type=...  43.4 us
    all_gather x2, waiting for transfers between devices, gather_attn(): lax.all_gather(jnp.where(side == 0, zero, one), BOTH, axis=0, tiled=False)  41.2 us
    unnamed x265, local copies, waits for them, and re-layouts  32.2 us
  transfers between devices with their start and end apart: 22, of which 10 were waited for; matrix products, arithmetic and copies ran while one was open for 36% of the time, Pallas kernels for 0%

commit v1 on v0

--- a/solution.py
+++ b/solution.py
@@ -297,7 +297,7 @@
     ge0, gs0 = reduce_ffn(dffn0)
     gh0, gp0 = reduce_attn(dattn0)
     flat = jnp.concatenate([small[k] for small in (small0, small1) for k in SMALL])
-    flat = lax.psum(flat, ("dp", "span", "tensor"))
+    flat = jnp.sum(lax.all_gather(flat, ("dp", "span", "tensor")), axis=0)
     sizes = [small0[k].shape[0] for k in SMALL] * 2
     cuts = []
     at = 0

time: 992 us -> 922 us (0.929)
  waiting for transfers between devices: 462 us -> 386 us
    psum x1 -> x0, waiting for transfers between devices: 71.1 us -> none  [shards(): flat = lax.psum(flat, ('dp', 'span', 'tensor'))]
    all_to_all x4, waiting for transfers between devices: 10.5 us -> 0.36 us  [to_places(): lax.all_to_all(values[None], 'tensor', split_axis=1, concat_axis=0, tiled...]
    unnamed x265 -> x255, local copies, waits for them, and re-layouts: 32.2 us -> 31 us
  transfers between devices with their start and end apart: 22 -> 22, of which waited for: 10 -> 9; matrix products, arithmetic and copies ran while one was open for 36% -> 40% of each run, Pallas kernels for 0% -> 0%
where the time goes in v1:
time: 922 us; the launch traced here: 916 us
  waiting for transfers between devices  386 us (42%)
  matrix products  184 us (20%)
  other arithmetic  103 us (11%)
  local copies, waits for them, and re-layouts  101 us (11%)
  blocking collectives  85.4 us (9%)
  starting transfers between devices  36.7 us (4%)
  between operations  19.6 us (2%)
    reduce_scatter x2, waiting for transfers between devices, reduce_ffn(): part = lax.psum_scatter(packed, BOTH, scatter_dimension=0, tiled=False)  139 us
    psum x1, waiting for transfers between devices, reduce_attn(): part = lax.psum(part, 'dp')  134 us
    all_gather x1, blocking collectives, shards(): anchors = lax.all_gather(cls, ('dp', 'span', 'tensor'), axis=0, tiled=False)  69.3 us
    all_gather x2, waiting for transfers between devices, gather_ffn(): lax.all_gather(jnp.where(side == 0, w_expand[l], w_shrink[l]), BOTH, axis...  56.6 us
    dot_general x26, matrix products, mm(): lax.dot_general(a, b, (((ca,), (cb,)), ((), ())), preferred_element_type=...  47.8 us
    all_gather x2, waiting for transfers between devices, gather_attn(): lax.all_gather(jnp.where(side == 0, zero, one), BOTH, axis=0, tiled=False)  41.1 us
    unnamed x255, local copies, waits for them, and re-layouts  31 us
    reshape x2, local copies, waits for them, and re-layouts, reduce_ffn(): packed = jnp.stack(grads).reshape(2 * tensor_count, width, ff_cols)  26.1 us
  transfers between devices with their start and end apart: 22, of which 9 were waited for; matrix products, arithmetic and copies ran while one was open for 40% of the time, Pallas kernels for 0%

profile of v1, /device:TPU:0, one launch (start us, length us, event | category | flops | bytes accessed | tf_op | source)
XLA Modules:
  0.0 916.4 jit_solution(13287772961196696378)
XLA Ops:
  12.7 3.3 slice_select_fusion
  16.1 5.3 all-to-all-start.5
  25.8 16.1 %all-gather.5 = bf16[4,1,2304]{2,1,0:T(2,128)(2,1)S(1)} all-gather(bf16[1,1,2304]{2,1,0:T(2,128)(2,1)S(1)} %reshape.547), channel_id=3, replica_groups=mesh['dp'=4,'span'=2,'tensor'=4] {'tensor'}, dimensions={0}, use_global_device_ids=true | all-gather | bytes 23040 | tf_op jit(solution)/shard_map/all_gather | solution.py:198
  44.3 3.5 all-to-all-start
  49.3 20.0 %all-gather.29.cloned.1.call-done = bf16[16,192,768]{2,1,0:T(8,128)(2,1)} async-done(((bf16[2,192,768]{2,1,0:T(8,128)(2,1)}), bf16[16,192,768]{2,1,0:T(8,128)(2,1)}) %all-gather.29.cloned.1.call-update) | async-done | bytes 4718608 | tf_op jit(solution)/shard_map/all_gather | solution.py:180
  69.3 4.2 fusion.150
  73.5 4.4 all-to-all-start.2
  86.4 2.6 fusion
  90.9 3.6 fusion.69
  96.6 21.0 %all-gather.31.cloned.1.call-done = bf16[16,192,768]{2,1,0:T(8,128)(2,1)} async-done(((bf16[2,192,768]{2,1,0:T(8,128)(2,1)}), bf16[16,192,768]{2,1,0:T(8,128)(2,1)}) %all-gather.31.cloned.1.call-update) | async-done | bytes 4718608 | tf_op jit(solution)/shard_map/all_gather | solution.py:180
  117.7 4.6 fusion.149
  122.3 56.6 %all-gather.17.cloned.1.call-done = bf16[8,768,768]{2,1,0:T(8,128)(2,1)} async-done(((bf16[1,768,768]{2,1,0:T(8,128)(2,1)}), bf16[8,768,768]{2,1,0:T(8,128)(2,1)}) %all-gather.17.cloned.1.call-update) | async-done | bytes 9437200 | tf_op jit(solution)/shard_map/all_gather | solution.py:191
  178.8 7.2 fusion.25
  186.1 2.8 fusion.158
  189.6 69.3 %all-gather.6 = bf16[32,4,768]{2,1,0:T(4,128)(2,1)S(1)} all-gather(bf16[1,4,768]{2,1,0:T(4,128)(2,1)S(1)} %fusion.74), channel_id=5, replica_groups=mesh['dp'=4,'span'=2,'tensor'=4] {'dp','span','tensor'}, dimensions={0}, use_global_device_ids=true | all-gather | bytes 202752 | tf_op jit(solution)/shard_map/all_gather | solution.py:243
  259.8 4.2 all-to-all-start.4
  264.1 2.6 fusion.75
  270.6 2.6 add_convert_fusion.2
  274.4 3.2 convolution_convert_fusion.10
  282.9 2.6 fusion.1
  287.3 3.8 fusion.68
  291.1 2.5 fusion.159
  295.0 5.5 fusion.21
  300.5 2.8 fusion.160
  308.0 4.9 fusion.36
  312.9 9.8 %multiply_reduce_fusion.3 = (f32[768]{0:T(1024)}, f32[512]{0:T(512)S(1)}, f32[512]{0:T(512)S(1)}, f32[768]{0:T(1024)}, f32[512,768]{1,0:T(8,128)S(1)}) fusion(f32[512,768]{1,0:T(8,128)S(1)} %get-tuple-element.135, f32[512]{0:T(512)S(1)} %add_rsqrt_fusion.1, f32[512]{0:T(512)S(1)} %broadcast_multiply_fusion.8, f32[768]{0:T(1024)S(1)} %get-tuple-element.42, ...), kind=kOutput, calls=%fused_computation.91 | convolution fusion | flops 2424567296 | bytes 18891776 | tf_op jit(solution)/shard_map/tqf,tdf->qd/dot_general | solution.py:111
  322.8 2.6 fusion.143
  331.2 9.6 %convert_reduce_fusion = (f32[12,64]{1,0:T(8,128)}, bf16[12,64,512]{2,1,0:T(8,128)(2,1)}) fusion(bf16[512,12,64]{0,2,1:T(8,128)(2,1)} %bitcast.410, f32[12,512]{1,0:T(8,128)S(1)} %log_add_fusion.1, f32[12,512,512]{1,2,0:T(8,128)} %copy-done.1, pred[512,512]{0,1:T(8,128)(4,1)S(1)} %broadcast_compare_fusion), kind=kOutput, calls=%fused_computation.92 | convolution fusion | flops 416414976 | bytes 14445568 | tf_op jit(solution)/shard_map/hqk,qhd->khd/dot_general | solution.py:65
  340.8 9.6 %multiply_reduce_fusion.1 = (f32[12,512]{1,0:T(8,128)S(1)}, f32[12,512,512]{1,2,0:T(8,128)}) fusion(f32[12,512]{1,0:T(8,128)S(1)} %log_add_fusion.1, f32[12,512,512]{1,2,0:T(8,128)} %copy-done.1, pred[512,512]{0,1:T(8,128)(4,1)S(1)} %broadcast_compare_fusion, bf16[512,12,64]{0,2,1:T(8,128)(2,1)S(1)} %bitcast.411, bf16[512,12,64]{0,2,1:T(8,128)(2,1)S(1)} %bitcast.407), kind=kOutput, calls=%fused_computation.4 | convolution fusion | flops 418375680 | bytes 27049984 | tf_op jit(solution)/shard_map/qhd,khd->hqk/dot_general | solution.py:60
  350.4 7.1 multiply_convert_fusion.1
  372.6 2.6 copy.201
  377.1 4.7 add_add_fusion
  381.8 4.0 multiply_reduce_fusion.4
  386.6 8.0 fusion.38
  394.6 3.1 multiply_reduce_fusion.5
  403.7 8.3 convert_reduce_fusion.2
  413.7 11.2 %multiply_reduce_fusion = (f32[12,512]{1,0:T(8,128)S(1)}, f32[12,512,512]{1,2,0:T(8,128)}) fusion(f32[12,512]{1,0:T(8,128)S(1)} %copy-done.63, f32[12,512,512]{1,2,0:T(8,128)} %copy-done, pred[512,512]{0,1:T(8,128)(4,1)S(1)} %broadcast_compare_fusion, bf16[512,12,64]{0,2,1:T(8,128)(2,1)S(1)} %bitcast.409, bf16[512,12,64]{0,2,1:T(8,128)(2,1)S(1)} %bitcast.439), kind=kOutput, calls=%fused_computation.1 | convolution fusion | flops 418375680 | bytes 27049984 | tf_op jit(solution)/shard_map/qhd,khd->hqk/dot_general | solution.py:60
  425.2 7.1 multiply_convert_fusion
  439.8 2.6 copy.200
  442.8 7.4 convert_bitcast_fusion
  450.2 8.4 convert_bitcast_fusion.1
  458.6 8.4 pad_maximum_fusion.1
  467.0 12.7 %copy.209 = bf16[8,768,768]{2,1,0:T(8,128)(2,1)} copy(bf16[8,768,768]{1,2,0:T(8,128)(2,1)} %bitcast.378) | data formatting | bytes 18874368 | tf_op jit(solution)/shard_map/reshape | solution.py:289
  480.2 7.3 convert_bitcast_fusion.2
  487.6 7.7 convert_bitcast_fusion.3
  495.3 8.3 pad_maximum_fusion
  503.6 13.4 %copy.205 = bf16[8,768,768]{2,1,0:T(8,128)(2,1)} copy(bf16[8,768,768]{1,2,0:T(8,128)(2,1)} %bitcast.379) | data formatting | bytes 18874368 | tf_op jit(solution)/shard_map/reshape | solution.py:289
  517.1 58.3 %reduce-scatter.11.cloned.1.call-done = bf16[1,768,768]{2,1,0:T(8,128)(2,1)} async-done(((bf16[8,768,768]{2,1,0:T(8,128)(2,1)}), bf16[1,768,768]{2,1,0:T(8,128)(2,1)}) %reduce-scatter.11.cloned.1.call-update) | async-done | bytes 1179664 | tf_op jit(solution)/shard_map/reduce_scatter | solution.py:290
  575.4 80.4 %reduce-scatter.9.cloned.1.call-done = bf16[1,768,768]{2,1,0:T(8,128)(2,1)} async-done(((bf16[8,768,768]{2,1,0:T(8,128)(2,1)}), bf16[1,768,768]{2,1,0:T(8,128)(2,1)}) %reduce-scatter.9.cloned.1.call-update) | async-done | bytes 1179664 | tf_op jit(solution)/shard_map/reduce_scatter | solution.py:290
  657.8 134.5 %all-reduce.3.cloned.1.call-done = (bf16[1,2,192,768]{3,2,1,0:T(8,128)(2,1)}, bf16[1,2,192,768]{3,2,1,0:T(8,128)(2,1)}, bf16[1,768,768]{2,1,0:T(8,128)(2,1)}, bf16[1,768,768]{2,1,0:T(8,128)(2,1)}) async-done(((bf16[1,2,192,768]{3,2,1,0:T(8,128)(2,1)}, bf16[1,2,192,768]{3,2,1,0:T(8,128)(2,1)}, bf16[1,768,768]{2,1,0:T(8,128)(2,1)}, bf16[1,768,768]{2,1,0:T(8,128)(2,1)}), (bf16[1,2,192,768]{3,2,1,0:T(8,128)(2,1)}, ...) | async-done | bytes 3538960 | tf_op jit(solution)/shard_map/psum | solution.py:283
  795.8 6.3 reduce.44
  804.0 4.4 all-to-all-start.1
  810.8 6.3 reduce.45
  819.4 4.2 all-to-all-start.3
  824.0 3.6 fusion.163
  829.0 6.3 reduce.47
  837.4 4.5 all-to-all-start.7
  846.6 5.4 reduce.46
  853.1 4.2 all-to-all-start.6
  883.9 3.4 all-gather.25.cloned.1.call-done
  887.3 3.4 fusion.151
  890.7 10.2 %all-gather.27.cloned.1.call-done = bf16[2,768,768]{2,1,0:T(8,128)(2,1)} async-done(((bf16[1,768,768]{2,1,0:T(8,128)(2,1)}), bf16[2,768,768]{2,1,0:T(8,128)(2,1)}) %all-gather.27.cloned.1.call-update) | async-done | bytes 2359312 | tf_op jit(solution)/shard_map/all_gather | solution.py:292
  903.2 2.5 pad_maximum_fusion.5
  905.7 2.5 pad_maximum_fusion.4
  (462 shorter events, 133.6 us)
Async XLA Ops:
  7.2 62.2 %all-gather.29.cloned.1.call-start = ((), (), s32[]{:S(2)}) async-start(), calls=%async_computation.22 | async-start | bytes 5308416 | tf_op jit(solution)/shard_map/all_gather | solution.py:180
  10.8 106.8 %all-gather.31.cloned.1.call-start = ((), (), s32[]{:S(2)}) async-start(), calls=%async_computation.23 | async-start | bytes 5308416 | tf_op jit(solution)/shard_map/all_gather | solution.py:180
  11.8 167.0 %all-gather.17.cloned.1.call-start = ((), (), s32[]{:S(2)}) async-start(), calls=%async_computation.12 | async-start | bytes 10616832 | tf_op jit(solution)/shard_map/all_gather | solution.py:191
  16.0 8.3 copy-start.96
  16.0 8.4 copy-start.95
  16.0 8.5 copy-start.88
  16.0 9.1 copy-start.78
  16.1 9.1 copy-start.79
  16.1 9.7 %copy-start.66 = (bf16[2,2,768]{2,1,0:T(2,128)(2,1)S(1)}, bf16[2,2,768]{2,1,0:T(2,128)(2,1)}, u32[]{:S(2)}) copy-start(bf16[2,2,768]{2,1,0:T(2,128)(2,1)} %param.26) | copy-start | bytes 18436
  16.1 26.7 %copy-start.67 = (bf16[2,2,768]{2,1,0:T(2,128)(2,1)S(1)}, bf16[2,2,768]{2,1,0:T(2,128)(2,1)}, u32[]{:S(2)}) copy-start(bf16[2,2,768]{2,1,0:T(2,128)(2,1)} %param.27) | copy-start | bytes 18436
  16.1 28.2 %all-to-all-start.5 = ((bf16[4,128,768]{2,1,0:T(8,128)(2,1)}), bf16[4,128,768]{2,1,0:T(8,128)(2,1)S(1)}, u32[]{:S(2)}, u32[]{:S(2)}) async-start(bf16[4,128,768]{2,1,0:T(8,128)(2,1)} %bitcast.446), calls=%async_computation.5 | async-start | bytes 1572864 | tf_op jit(solution)/shard_map/all_to_all | solution.py:144
  21.4 273.5 %all-gather.19.cloned.1.call-start = ((), (), s32[]{:S(2)}) async-start(), calls=%async_computation.13 | async-start | bytes 10616832 | tf_op jit(solution)/shard_map/all_gather | solution.py:191
  22.8 166.4 %copy-start.85 = (s32[4]{0:T(128)}, s32[4]{0:T(128)S(1)}, u32[]{:S(2)}) copy-start(s32[4]{0:T(128)S(1)} %bitcast_subtract_fusion) | copy-start | bytes 52
  23.7 267.4 %copy-start.90 = (pred[512]{0:T(512)(128)(4,1)}, pred[512]{0:T(512)(128)(4,1)S(1)}, u32[]{:S(2)}) copy-start(pred[512]{0:T(512)(128)(4,1)S(1)} %broadcast_compare_fusion.1) | copy-start | bytes 1540
  43.4 142.6 %copy-start.74 = (f32[768]{0:T(1024)}, f32[768]{0:T(1024)S(1)}, u32[]{:S(2)}) copy-start(f32[768]{0:T(1024)S(1)} %get-tuple-element.45) | copy-start | bytes 9220
  44.0 134.8 %copy-start.81 = (f32[4,768]{1,0:T(4,128)}, f32[4,768]{1,0:T(4,128)S(1)}, u32[]{:S(2)}) copy-start(f32[4,768]{1,0:T(4,128)S(1)} %get-tuple-element.121) | copy-start | bytes 36868
  44.3 29.3 %copy-start.6 = (bf16[4,128,768]{2,1,0:T(8,128)(2,1)}, bf16[4,128,768]{2,1,0:T(8,128)(2,1)S(1)}, u32[]{:S(2)}) copy-start(bf16[4,128,768]{2,1,0:T(8,128)(2,1)S(1)} %all-to-all-done.5) | copy-start | bytes 2359300
  44.3 29.3 %all-to-all-start = ((bf16[4,128,768]{2,1,0:T(8,128)(2,1)}), bf16[4,128,768]{2,1,0:T(8,128)(2,1)S(1)}, u32[]{:S(2)}, u32[]{:S(2)}) async-start(bf16[4,128,768]{2,1,0:T(8,128)(2,1)} %bitcast), calls=%async_computation | async-start | bytes 1572864 | tf_op jit(solution)/shard_map/all_to_all | solution.py:144
  73.5 9.0 copy-start.18
  73.5 186.3 %all-to-all-start.2 = ((bf16[4,128,768]{2,1,0:T(8,128)(2,1)}), bf16[4,128,768]{2,1,0:T(8,128)(2,1)}, u32[]{:S(2)}, u32[]{:S(2)}) async-start(bf16[4,128,768]{2,1,0:T(8,128)(2,1)} %bitcast.29), calls=%async_computation.2 | async-start | bytes 1572864 | tf_op jit(solution)/shard_map/all_to_all | solution.py:144
  95.5 90.5 %copy-start.2 = (f32[512,768]{1,0:T(8,128)}, f32[512,768]{1,0:T(8,128)S(1)}, u32[]{:S(2)}) copy-start(f32[512,768]{1,0:T(8,128)S(1)} %get-tuple-element.127) | copy-start | bytes 4718596
  259.0 7.6 copy-start.33
  259.8 122.0 %all-to-all-start.4 = ((bf16[4,128,768]{2,1,0:T(8,128)(2,1)}), bf16[4,128,768]{2,1,0:T(8,128)(2,1)}, u32[]{:S(2)}, u32[]{:S(2)}) async-start(bf16[4,128,768]{2,1,0:T(8,128)(2,1)} %bitcast.54), calls=%async_computation.4 | async-start | bytes 1572864 | tf_op jit(solution)/shard_map/all_to_all | solution.py:144
  264.0 253.0 %reduce-scatter.7.cloned.1.call-start = ((), (), s32[]{:S(2)}) async-start(), calls=%async_computation.16 | async-start | bytes 5308416 | tf_op jit(solution)/shard_map/reduce_scatter | solution.py:282
  270.6 10.1 %copy-start.11 = (bf16[512,768]{0,1:T(8,128)(2,1)}, bf16[512,768]{0,1:T(8,128)(2,1)S(1)}, u32[]{:S(2)}) copy-start(bf16[512,768]{0,1:T(8,128)(2,1)S(1)} %copy.183) | copy-start | bytes 2359300
  280.5 14.3 %copy-start.46 = (f32[64,64]{1,0:T(8,128)}, f32[64,64]{1,0:T(8,128)S(1)}, u32[]{:S(2)}) copy-start(f32[64,64]{1,0:T(8,128)S(1)} %get-tuple-element.140) | copy-start | bytes 49156
  293.6 19.3 %copy-start.4 = (f32[512,768]{1,0:T(8,128)}, f32[512,768]{1,0:T(8,128)S(1)}, u32[]{:S(2)}) copy-start(f32[512,768]{1,0:T(8,128)S(1)} %get-tuple-element.135) | copy-start | bytes 4718596
  294.7 28.0 %copy-start.68 = (f32[512]{0:T(512)}, f32[512]{0:T(512)S(1)}, u32[]{:S(2)}) copy-start(f32[512]{0:T(512)S(1)} %add_rsqrt_fusion.1) | copy-start | bytes 6148
  312.9 9.8 %copy-start.15 = (f32[4,768,512]{1,2,0:T(8,128)}, f32[4,768,512]{1,2,0:T(8,128)S(1)}, u32[]{:S(2)}) copy-start(f32[4,768,512]{1,2,0:T(8,128)S(1)} %get-tuple-element.141) | copy-start | bytes 18874372
  312.9 9.8 %copy-start.27 = (bf16[4,512,768]{2,1,0:T(8,128)(2,1)}, bf16[4,512,768]{2,1,0:T(8,128)(2,1)S(1)}, u32[]{:S(2)}) copy-start(bf16[4,512,768]{2,1,0:T(8,128)(2,1)S(1)} %get-tuple-element.56) | copy-start | bytes 9437188
  331.2 9.6 %copy-start.22 = (bf16[512,768]{0,1:T(8,128)(2,1)S(1)}, bf16[512,768]{0,1:T(8,128)(2,1)}, u32[]{:S(2)}) copy-start(bf16[512,768]{0,1:T(8,128)(2,1)} %copy.182) | copy-start | bytes 2359300
  331.2 9.6 %copy-start.24 = (bf16[512,768]{0,1:T(8,128)(2,1)S(1)}, bf16[512,768]{0,1:T(8,128)(2,1)}, u32[]{:S(2)}) copy-start(bf16[512,768]{0,1:T(8,128)(2,1)} %copy.188) | copy-start | bytes 2359300
  331.2 19.2 %slice-start.3 = ((s8[12582912]{0:T(1024)(128)(4,1)}), s8[4194304]{0:T(1024)(128)(4,1)S(1)}, s32[]{:S(2)}) async-start(s8[12582912]{0:T(1024)(128)(4,1)} %bitcast.376), calls=%async_computation.29 | async-start | bytes 8388608
  331.2 19.2 %slice-start.4 = ((s8[12582912]{0:T(1024)(128)(4,1)}), s8[4194304]{0:T(1024)(128)(4,1)S(1)}, s32[]{:S(2)}) async-start(s8[12582912]{0:T(1024)(128)(4,1)} %bitcast.376), calls=%async_computation.30 | async-start | bytes 8388608
  340.8 9.7 %slice-start.5 = ((s8[12582912]{0:T(1024)(128)(4,1)}), s8[4194304]{0:T(1024)(128)(4,1)S(1)}, s32[]{:S(2)}) async-start(s8[12582912]{0:T(1024)(128)(4,1)} %bitcast.376), calls=%async_computation.31 | async-start | bytes 8388608
  375.2 141.9 %reduce-scatter.5.cloned.1.call-start = ((), (), s32[]{:S(2)}) async-start(), calls=%async_computation.14 | async-start | bytes 5308416 | tf_op jit(solution)/shard_map/reduce_scatter | solution.py:282
  381.8 12.8 %slice-start.6 = ((s8[9437184]{0:T(1024)(128)(4,1)}), s8[4194304]{0:T(1024)(128)(4,1)S(1)}, s32[]{:S(2)}) async-start(s8[9437184]{0:T(1024)(128)(4,1)} %bitcast.475), calls=%async_computation.32 | async-start | bytes 8388608
  386.4 8.2 copy-start.36
  386.6 8.0 copy-start.3
  386.6 8.0 slice-start.7
  386.6 8.1 slice-start.8
  403.7 9.2 %copy-start.59 = (bf16[4,128,768]{2,1,0:T(8,128)(2,1)S(1)}, bf16[4,128,768]{2,1,0:T(8,128)(2,1)}, u32[]{:S(2)}) copy-start(bf16[4,128,768]{2,1,0:T(8,128)(2,1)} %copy-done.56) | copy-start | bytes 2359300
  403.7 10.0 %copy-start.23 = (bf16[512,768]{0,1:T(8,128)(2,1)S(1)}, bf16[512,768]{0,1:T(8,128)(2,1)}, u32[]{:S(2)}) copy-start(bf16[512,768]{0,1:T(8,128)(2,1)} %copy.194) | copy-start | bytes 2359300
  403.7 10.0 %copy-start.49 = (bf16[768,512]{1,0:T(8,128)(2,1)S(1)}, bf16[768,512]{1,0:T(8,128)(2,1)}, u32[]{:S(2)}) copy-start(bf16[768,512]{1,0:T(8,128)(2,1)} %add_convert_fusion.4) | copy-start | bytes 2359300
  412.8 12.0 %slice-start = ((s8[12582912]{0:T(1024)(128)(4,1)}), s8[4194304]{0:T(1024)(128)(4,1)S(1)}, s32[]{:S(2)}) async-start(s8[12582912]{0:T(1024)(128)(4,1)} %bitcast.374), calls=%async_computation.26 | async-start | bytes 8388608
  413.6 11.2 %slice-start.1 = ((s8[12582912]{0:T(1024)(128)(4,1)}), s8[4194304]{0:T(1024)(128)(4,1)S(1)}, s32[]{:S(2)}) async-start(s8[12582912]{0:T(1024)(128)(4,1)} %bitcast.374), calls=%async_computation.27 | async-start | bytes 8388608
  413.7 11.5 %slice-start.2 = ((s8[12582912]{0:T(1024)(128)(4,1)}), s8[4194304]{0:T(1024)(128)(4,1)S(1)}, s32[]{:S(2)}) async-start(s8[12582912]{0:T(1024)(128)(4,1)} %bitcast.374), calls=%async_computation.28 | async-start | bytes 8388608
  442.4 7.7 copy-start.69
  442.4 7.7 copy-start.77
  442.4 133.0 %reduce-scatter.11.cloned.1.call-start = ((), (), s32[]{:S(2)}) async-start(), calls=%async_computation.20 | async-start | bytes 10616832 | tf_op jit(solution)/shard_map/reduce_scatter | solution.py:290
  442.7 7.4 copy-start.5
  442.7 7.4 copy-start.28
  479.7 7.9 copy-start.75
  479.7 176.1 %reduce-scatter.9.cloned.1.call-start = ((), (), s32[]{:S(2)}) async-start(), calls=%async_computation.18 | async-start | bytes 10616832 | tf_op jit(solution)/shard_map/reduce_scatter | solution.py:290
  517.0 275.3 %all-reduce.3.cloned.1.call-start = ((), (), s32[]{:S(2)}) async-start(), calls=%async_computation.25 | async-start | bytes 7077888 | tf_op jit(solution)/shard_map/psum | solution.py:283
  655.9 214.7 %all-gather.33.cloned.1.call-start = ((), (), s32[]{:S(2)}) async-start(), calls=%async_computation.24 | async-start | bytes 2433024 | tf_op jit(solution)/shard_map/all_gather | solution.py:300
  657.8 219.4 %all-gather.21.cloned.1.call-start = ((), (), s32[]{:S(2)}) async-start(), calls=%async_computation.15 | async-start | bytes 1769472 | tf_op jit(solution)/shard_map/all_gather | solution.py:284
  792.3 86.3 %all-gather.23.cloned.1.call-start = ((), (), s32[]{:S(2)}) async-start(), calls=%async_computation.17 | async-start | bytes 1769472 | tf_op jit(solution)/shard_map/all_gather | solution.py:284
  804.0 15.4 %all-to-all-start.1 = ((bf16[4,2,49152]{2,1,0:T(2,128)(2,1)}), bf16[4,2,49152]{2,1,0:T(2,128)(2,1)}, u32[]{:S(2)}, u32[]{:S(2)}) async-start(bf16[4,2,49152]{2,1,0:T(2,128)(2,1)} %reshape.578), calls=%async_computation.1 | async-start | bytes 1572864 | tf_op jit(solution)/shard_map/all_to_all | solution.py:148
  819.4 18.0 %all-to-all-start.3 = ((bf16[4,2,49152]{2,1,0:T(2,128)(2,1)}), bf16[4,2,49152]{2,1,0:T(2,128)(2,1)}, u32[]{:S(2)}, u32[]{:S(2)}) async-start(bf16[4,2,49152]{2,1,0:T(2,128)(2,1)} %reshape.580), calls=%async_computation.3 | async-start | bytes 1572864 | tf_op jit(solution)/shard_map/all_to_all | solution.py:148
  823.7 63.6 %all-gather.25.cloned.1.call-start = ((), (), s32[]{:S(2)}) async-start(), calls=%async_computation.19 | async-start | bytes 3538944 | tf_op jit(solution)/shard_map/all_gather | solution.py:292
  837.4 15.7 %all-to-all-start.7 = ((bf16[4,2,49152]{2,1,0:T(2,128)(2,1)}), bf16[4,2,49152]{2,1,0:T(2,128)(2,1)S(1)}, u32[]{:S(2)}, u32[]{:S(2)}) async-start(bf16[4,2,49152]{2,1,0:T(2,128)(2,1)} %reshape.584), calls=%async_computation.7 | async-start | bytes 1572864 | tf_op jit(solution)/shard_map/all_to_all | solution.py:148
  853.1 15.8 %all-to-all-start.6 = ((bf16[4,2,49152]{2,1,0:T(2,128)(2,1)}), bf16[4,2,49152]{2,1,0:T(2,128)(2,1)S(1)}, u32[]{:S(2)}, u32[]{:S(2)}) async-start(bf16[4,2,49152]{2,1,0:T(2,128)(2,1)} %reshape.582), calls=%async_computation.6 | async-start | bytes 1572864 | tf_op jit(solution)/shard_map/all_to_all | solution.py:148
  857.3 43.6 %all-gather.27.cloned.1.call-start = ((), (), s32[]{:S(2)}) async-start(), calls=%async_computation.21 | async-start | bytes 3538944 | tf_op jit(solution)/shard_map/all_gather | solution.py:292
  (69 other events, 199.1 us)
Sparse Core Ops, SparseCore 0:
  11.0 58.3 all-gather.28
  71.8 45.8 all-gather.30
  120.1 58.6 all-gather.16
  181.2 60.4 all-gather.18
  375.3 52.3 reduce-scatter.6
  442.5 52.5 reduce-scatter.4
  498.6 76.8 reduce-scatter.10
  578.9 76.8 reduce-scatter.8
  658.4 133.8 all-reduce.2
  795.6 56.2 all-gather.32
  853.4 8.3 all-gather.20
  863.2 10.3 all-gather.22
  875.1 12.1 all-gather.24
  888.7 12.1 all-gather.26
